TPU v7x, 128 devices: a whole 4x4x4 slice. The times are simulated.
128 devices in a mesh: copy: 2 (over x_hi), ctx: 32 (over y, z, x_lo), tp: 2 (over core).
Axes of the slice: x: 4 (x_hi: 2, x_lo: 2; x = x_hi * 2 + x_lo), y: 4, z: 4, core: 2. Of those that a mesh axis runs over, the one named last changes fastest.
Arguments:
- clean_tokens: bfloat16 [8192, 4096], P('ctx', 'copy'), may hold values from -36 to 36
- norm_gain: bfloat16 [4096], replicated, may hold values from 0.5 to 1.5
- mask_embed: bfloat16 [4096], replicated, may hold values from -6 to 6
- time_shift: float32 [4096], replicated, may hold values from -0.5 to 0.5
- w_query: bfloat16 [4096, 2048], P(None, 'tp'), may hold values from -0.09375 to 0.09375
- w_key: bfloat16 [4096, 512], P(None, 'tp'), may hold values from -0.09375 to 0.09375
- w_value: bfloat16 [4096, 512], P(None, 'tp'), may hold values from -0.09375 to 0.09375
- w_out: bfloat16 [2048, 4096], P('tp'), may hold values from -0.125 to 0.125
- q_gain: float32 [128], replicated, may hold values from 2 to 3
- k_gain: float32 [128], replicated, may hold values from 0.5 to 1.5
- masked: int32 [2, 8192], P('copy', 'ctx'), may hold values 0 or 1
- block_live: int32 [2, 128], P('copy', 'ctx'), may hold values 0 or 1
- timesteps: int32 [2], P('copy'), may hold values from 1 to 1000
Outputs:
- clean_out: bfloat16 [8192, 4096], P('ctx', 'tp')
- noised_out: bfloat16 [2, 8192, 4096], P('copy', 'ctx', 'tp')
All inputs are finite; a program needn't handle non-finite values. No bound on the sum of `masked` or of `block_live` on one device may be relied on, other than what follows from the above.
Results may differ from a plain program's by a relative error of at most 0.012.
The roundings to bfloat16 on the way count: a program that leaves them out, or rounds other values in their place, can miss the bound.
Values may be sent and summed in bfloat16 or wider, within the bound.
A program may use at most 320 MiB of HBM per device.

v0:
```python
import math
import jax
import jax.numpy as jnp
from jax import lax
from jax.sharding import PartitionSpec as P

HD = 128
BLK = 64
TSTEPS = 1000
EPS = 1e-06


def inverse_rms(values):
    return lax.rsqrt(jnp.mean(values * values, axis=-1, keepdims=True) + EPS)


def key_terms(state, queries, query_start, key_piece, value_piece, key_start):
    numerator, denominator = state
    streams_count, row_count, kv_local, group_size, head_dim = queries.shape
    piece_rows = key_piece.shape[0]
    key_heads = key_piece.reshape(piece_rows, kv_local, head_dim)
    value_heads = value_piece.reshape(piece_rows, kv_local, head_dim)

    def compute():
        scores = jnp.einsum(
            "srhgd,khd->srhgk", queries, key_heads, preferred_element_type=jnp.float32
        ) * (1.0 / math.sqrt(head_dim))
        query_blocks = (query_start + jnp.arange(row_count, dtype=jnp.int32)) // BLK
        key_blocks = jnp.arange(piece_rows, dtype=jnp.int32) // BLK
        offset = jnp.minimum(jnp.arange(streams_count, dtype=jnp.int32), 1)
        allowed = key_blocks[None, None, :] + offset[:, None, None] <= query_blocks[None, :, None]
        weights = jnp.where(allowed[:, :, None, None, :], jnp.exp(scores), 0.0)
        updated = jnp.einsum(
            "srhgk,khd->srhgd",
            weights.astype(jnp.bfloat16),
            value_heads,
            preferred_element_type=jnp.float32,
        )
        return (updated, jnp.sum(weights, axis=4))

    def unchanged():
        return (numerator, denominator)

    needed = key_start // BLK <= (query_start + row_count - 1) // BLK
    return lax.cond(needed, compute, unchanged)


def own_block(queries, key_heads, value_heads):
    copies, row_count, kv_local, group_size, head_dim = queries.shape
    count_blocks = row_count // BLK
    query_blocks = queries.reshape(copies, count_blocks, BLK, kv_local, group_size, head_dim)
    key_blocks = key_heads.reshape(copies, count_blocks, BLK, kv_local, head_dim)
    value_blocks = value_heads.reshape(copies, count_blocks, BLK, kv_local, head_dim)
    scores = jnp.einsum(
        "cbqhgd,cbkhd->cbqhgk", query_blocks, key_blocks, preferred_element_type=jnp.float32
    ) * (1.0 / math.sqrt(head_dim))
    weights = jnp.exp(scores)
    numerator = jnp.einsum(
        "cbqhgk,cbkhd->cbqhgd",
        weights.astype(jnp.bfloat16),
        value_blocks,
        preferred_element_type=jnp.float32,
    )
    denominator = jnp.sum(weights, axis=5)
    return (
        numerator.reshape(copies, row_count, kv_local, group_size, head_dim),
        denominator.reshape(copies, row_count, kv_local, group_size),
    )


def on_device(
    clean_tokens,
    norm_gain,
    mask_embed,
    time_shift,
    w_query,
    w_key,
    w_value,
    w_out,
    q_gain,
    k_gain,
    masked,
    block_live,
    timesteps,
):
    features = lax.all_gather(clean_tokens, "copy", axis=1, tiled=True)
    local_rows = features.shape[0]
    width = features.shape[1]
    copies = masked.shape[0]
    streams_count = 1 + copies
    kv_local = w_key.shape[1] // HD
    heads_local = w_query.shape[1] // HD
    group_size = heads_local // kv_local
    features_wide = features.astype(jnp.float32)
    gain_wide = norm_gain.astype(jnp.float32)
    normed_clean = (features_wide * inverse_rms(features_wide) * gain_wide).astype(jnp.bfloat16)
    noisy_tokens = jnp.where(
        masked[:, :, None] == 1, mask_embed[None, None, :], features[None, :, :]
    )
    noisy_wide = noisy_tokens.astype(jnp.float32)
    condition = (
        1.0 + timesteps.astype(jnp.float32)[:, None, None] / TSTEPS * time_shift[None, None, :]
    )
    normed_noisy = (noisy_wide * inverse_rms(noisy_wide) * gain_wide * condition).astype(
        jnp.bfloat16
    )
    all_rows = jnp.concatenate([normed_clean[None], normed_noisy], axis=0).reshape(-1, width)
    query_wide = jnp.dot(all_rows, w_query, preferred_element_type=jnp.float32).reshape(
        streams_count, local_rows, kv_local, group_size, HD
    )
    queries = (query_wide * inverse_rms(query_wide) * q_gain).astype(jnp.bfloat16)
    key_wide = jnp.dot(all_rows, w_key, preferred_element_type=jnp.float32).reshape(
        streams_count, local_rows, kv_local, HD
    )
    key_heads = (key_wide * inverse_rms(key_wide) * k_gain).astype(jnp.bfloat16)
    value_heads = (
        jnp.dot(all_rows, w_value, preferred_element_type=jnp.float32)
        .astype(jnp.bfloat16)
        .reshape(streams_count, local_rows, kv_local, HD)
    )
    clean_keys = key_heads[0].reshape(local_rows, kv_local * HD)
    clean_values = value_heads[0].reshape(local_rows, kv_local * HD)
    position = lax.axis_index("ctx")
    first_row = position * local_rows
    groups = ((queries, first_row, key_heads[1:], value_heads[1:]),)
    initial = tuple(
        (
            (jnp.zeros(member[0].shape, jnp.float32), jnp.zeros(member[0].shape[:-1], jnp.float32))
            for member in groups
        )
    )
    piece = (
        lax.all_gather(clean_keys, "ctx", axis=0, tiled=True),
        lax.all_gather(clean_values, "ctx", axis=0, tiled=True),
    )
    key_start = jnp.int32(0)
    totals = tuple(
        (
            key_terms(
                initial[number], groups[number][0], groups[number][1], piece[0], piece[1], key_start
            )
            for number in range(len(groups))
        )
    )
    number = 0
    numerator, denominator = totals[number]
    member = groups[number]
    self_numerator, own_den = own_block(member[0][1:], member[2], member[3])
    numerator = jnp.concatenate([numerator[:1], numerator[1:] + self_numerator], axis=0)
    denominator = jnp.concatenate([denominator[:1], denominator[1:] + own_den], axis=0)
    results = (numerator / denominator[..., None]).astype(jnp.bfloat16)
    head_rows = results.reshape(streams_count * local_rows, heads_local * HD)
    mixed = lax.psum_scatter(
        jnp.dot(head_rows, w_out, preferred_element_type=jnp.float32),
        "tp",
        scatter_dimension=1,
        tiled=True,
    )
    clean_out = mixed[:local_rows].astype(jnp.bfloat16)
    live_rows = jnp.repeat(block_live, BLK, axis=1).astype(jnp.float32)
    noised_out = (
        mixed[local_rows:].reshape(copies, local_rows, -1) * live_rows[:, :, None]
    ).astype(jnp.bfloat16)
    return (clean_out, noised_out)


def solution(mesh):
    in_specs = (
        P("ctx", "copy"),
        P(),
        P(),
        P(),
        P(None, "tp"),
        P(None, "tp"),
        P(None, "tp"),
        P("tp", None),
        P(),
        P(),
        P("copy", "ctx"),
        P("copy", "ctx"),
        P("copy"),
    )
    out_specs = (P("ctx", "tp"), P("copy", "ctx", "tp"))
    return jax.shard_map(
        on_device, mesh=mesh, in_specs=in_specs, out_specs=out_specs, check_vma=False
    )
```

profile of v0, /device:TPU:1, one launch (start us, length us, event | category | flops | bytes accessed | tf_op | source)
XLA Modules:
  0.0 565.8 jit_solution(7580052467397267353)
XLA Ops:
  9.3 4.1 copy.93
  13.5 36.6 %all-gather.4.cloned.1.call-done = bf16[256,4096]{1,0:T(8,128)(2,1)} async-done(((bf16[256,2048]{1,0:T(8,128)(2,1)}), bf16[256,4096]{1,0:T(8,128)(2,1)}) %all-gather.4.cloned.1.call-update) | async-done | bytes 2097168 | tf_op jit(solution)/shard_map/all_gather | solution.py:86
  50.1 3.4 fusion.19
  53.5 4.2 fusion.31
  57.7 1.3 multiply_reduce_fusion.1
  59.8 0.7 copy.66
  60.7 2.6 pad_maximum_fusion
  63.3 1.3 convolution_convert_fusion
  65.3 11.4 %copy.94 = bf16[1024,4096]{1,0:T(8,128)(2,1)} copy(bf16[1024,4096]{0,1:T(8,128)(2,1)} %bitcast.72) | data formatting | bytes 16777216 | tf_op jit(solution)/shard_map/dot_general | solution.py:108
  76.9 8.2 %multiply_reduce_fusion = (f32[2,256,2,4]{1,3,2,0:T(4,128)S(1)}, f32[2,256,2,4,128]{4,1,3,2,0:T(8,128)S(1)}) fusion(bf16[2,4,128,4096,1]{3,2,1,0,4:T(8,128)(2,1)} %bitcast.73, bf16[1,256,4096]{2,1,0:T(8,128)(2,1)} %copy-done.4, bf16[1,256,4096]{2,1,0:T(8,128)(2,1)S(1)} %copy-done.3), kind=kOutput, calls=%fused_computation.50 | convolution fusion | flops 4304400384 | bytes 14696448 | tf_op jit(solution)/shard_map/dot_general | solution.py:108
  87.2 118.4 %all-gather.6.cloned.1.call-done = bf16[8192,256]{1,0:T(8,128)(2,1)} async-done(((bf16[256,256]{1,0:T(8,128)(2,1)}), bf16[8192,256]{1,0:T(8,128)(2,1)}) %all-gather.6.cloned.1.call-update) | async-done | bytes 4194320 | tf_op jit(solution)/shard_map/all_gather | solution.py:133
  205.6 168.3 %all-gather.8.cloned.1.call-done = bf16[8192,256]{1,0:T(8,128)(2,1)} async-done(((bf16[256,256]{1,0:T(8,128)(2,1)}), bf16[8192,256]{1,0:T(8,128)(2,1)}) %all-gather.8.cloned.1.call-update) | async-done | bytes 4194320 | tf_op jit(solution)/shard_map/all_gather | solution.py:134
  373.9 126.5 %conditional.1 = (f32[2,256,2,4,128]{4,1,3,0,2:T(8,128)S(1)}, f32[2,256,2,4]{1,3,0,2:T(4,128)S(1)}) conditional(s32[]{:T(128)} %convert_element_type.70, () %tuple.16, (s32[]{:T(128)}, bf16[8192,256]{1,0:T(8,128)(2,1)}, bf16[2,256,2,4,128]{4,1,3,2,0:T(8,128)(2,1)}, bf16[8192,256]{1,0:T(8,128)(2,1)}) %tuple.45), branch_computations={%region_4.5_spmd, %region_5.7_spmd} | conditional | flops 17385472000 | bytes 313739328 | solution.py:45
  374.1 7.8 %broadcast_compare_fusion = pred[2,256,8192]{1,2,0:T(8,128)(4,1)} fusion(s32[256]{0:T(256)S(1)} %and_select_fusion, s32[2,8192]{1,0:T(2,128)S(1)} %broadcast_add_fusion), kind=kLoop, calls=%fused_computation.5 | loop fusion | flops 4194304 | bytes 4260864 | tf_op jit(solution)/shard_map/cond/branch_1_fun/le | solution.py:31
  381.9 7.0 %reshape.217 = bf16[8192,2,128]{2,1,0:T(2,128)(2,1)} reshape(bf16[8192,256]{1,0:T(8,128)(2,1)} %get-tuple-element.11) | data formatting | bytes 8388608 | tf_op jit(solution)/shard_map/reshape | solution.py:21
  388.9 48.1 %fusion = (f32[2,256,2,4]{1,3,0,2:T(4,128)S(1)}, f32[2,8192,2,256,4]{3,1,4,2,0:T(8,128)}) fusion(pred[2,256,8192]{1,2,0:T(8,128)(4,1)} %broadcast_compare_fusion, bf16[2,256,2,4,128]{4,1,3,2,0:T(8,128)(2,1)S(1)} %copy-done.6, bf16[8192,2,128,1,1]{2,1,0,4,3:T(2,128)(2,1)} %bitcast.74), kind=kOutput, calls=%fused_computation.1 | convolution fusion | flops 8690593792 | bytes 143671296 | tf_op jit(solution)/shard_map/cond/branch_1_fun/srhgd,khd->srhgk/dot_general | solution.py:25
  437.0 6.9 %reshape.218 = bf16[8192,2,128]{2,1,0:T(2,128)(2,1)} reshape(bf16[8192,256]{1,0:T(8,128)(2,1)} %get-tuple-element.13) | data formatting | bytes 8388608 | tf_op jit(solution)/shard_map/reshape | solution.py:22
  443.9 56.5 %fusion.8 = f32[2,256,2,4,128]{4,1,3,0,2:T(8,128)S(1)} fusion(bf16[8192,2,128,1,1]{2,1,0,4,3:T(2,128)(2,1)} %bitcast.75, f32[2,8192,2,256,4]{3,1,4,2,0:T(8,128)} %get-tuple-element.39, pred[2,256,8192]{1,2,0:T(8,128)(4,1)} %broadcast_compare_fusion), kind=kOutput, calls=%fused_computation.9 | convolution fusion | flops 8690597888 | bytes 144703488 | tf_op jit(solution)/shard_map/cond/branch_1_fun/srhgk,khd->srhgd/dot_general | solution.py:33
  501.4 0.8 copy.80
  502.2 0.8 convert_element_type.83
  503.0 10.0 %fusion.47 = f32[512,4096]{1,0:T(8,128)} fusion(bf16[512,1024]{1,0:T(8,128)(2,1)S(1)} %convert_element_type.83, bf16[1024,4096]{1,0:T(8,128)(2,1)} %param.22), kind=kOutput, calls=%fused_computation.80 | convolution fusion | flops 4294967296 | bytes 17825792 | tf_op jit(solution)/shard_map/dot_general | solution.py:154
  513.8 40.0 %reduce-scatter.2.cloned.1.call-done = f32[512,2048]{1,0:T(8,128)} async-done(((f32[512,4096]{1,0:T(8,128)}), f32[512,2048]{1,0:T(8,128)}) %reduce-scatter.2.cloned.1.call-update) | async-done | bytes 4194320 | tf_op jit(solution)/shard_map/reduce_scatter | solution.py:153
  553.8 2.7 slice.66
  556.5 2.7 fusion.36
  (65 shorter events, 7.2 us)
Async XLA Ops:
  7.2 56.1 %copy-start = (bf16[4096,256]{1,0:T(8,128)(2,1)S(1)}, bf16[4096,256]{1,0:T(8,128)(2,1)}, u32[]{:S(2)}) copy-start(bf16[4096,256]{1,0:T(8,128)(2,1)} %param.21) | copy-start | bytes 6291460
  7.2 6.3 %copy-start.12 = (s32[1,256]{1,0:T(1,128)S(1)}, s32[1,256]{1,0:T(1,128)}, u32[]{:S(2)}) copy-start(s32[1,256]{1,0:T(1,128)} %param.25) | copy-start | bytes 3076
  7.2 6.3 %copy-start.9 = (f32[4096]{0:T(1024)S(1)}, f32[4096]{0:T(1024)}, u32[]{:S(2)}) copy-start(f32[4096]{0:T(1024)} %param.18) | copy-start | bytes 49156
  7.2 42.9 %copy-start.8 = (bf16[4096]{0:T(1024)(128)(2,1)S(1)}, bf16[4096]{0:T(1024)(128)(2,1)}, u32[]{:S(2)}) copy-start(bf16[4096]{0:T(1024)(128)(2,1)} %param.17) | copy-start | bytes 24580
  7.2 42.9 %all-gather.4.cloned.1.call-start = ((), (), s32[]{:S(2)}) async-start(), calls=%async_computation.1 | async-start | bytes 3145728 | tf_op jit(solution)/shard_map/all_gather | solution.py:86
  7.9 197.7 %all-gather.6.cloned.1.call-start = ((), (), s32[]{:S(2)}) async-start(), calls=%async_computation.2 | async-start | bytes 4325376 | tf_op jit(solution)/shard_map/all_gather | solution.py:133
  50.1 7.6 %copy-start.7 = (bf16[256,4096]{1,0:T(8,128)(2,1)S(1)}, bf16[256,4096]{1,0:T(8,128)(2,1)}, u32[]{:S(2)}) copy-start(bf16[256,4096]{1,0:T(8,128)(2,1)} %copy.93) | copy-start | bytes 6291460
  57.7 1.4 copy-start.2
  57.7 2.0 copy-start.4
  57.7 2.0 copy-start.10
  60.6 313.3 %all-gather.8.cloned.1.call-start = ((), (), s32[]{:S(2)}) async-start(), calls=%async_computation.3 | async-start | bytes 4325376 | tf_op jit(solution)/shard_map/all_gather | solution.py:134
  65.3 488.6 %reduce-scatter.2.cloned.1.call-start = ((), (), s32[]{:S(2)}) async-start(), calls=%async_computation.4 | async-start | bytes 12582912 | tf_op jit(solution)/shard_map/reduce_scatter | solution.py:153
  65.3 11.5 %copy-start.3 = (bf16[1,256,4096]{2,1,0:T(8,128)(2,1)S(1)}, bf16[1,256,4096]{2,1,0:T(8,128)(2,1)}, u32[]{:S(2)}) copy-start(bf16[1,256,4096]{2,1,0:T(8,128)(2,1)} %copy-done.2) | copy-start | bytes 6291460
  76.9 8.2 %copy-start.11 = (f32[128]{0:T(128)S(1)}, f32[128]{0:T(128)}, u32[]{:S(2)}) copy-start(f32[128]{0:T(128)} %param.23) | copy-start | bytes 1540
  85.8 1.0 copy-start.5
  381.9 7.0 %copy-start.6 = (bf16[2,256,2,4,128]{4,1,3,2,0:T(8,128)(2,1)S(1)}, bf16[2,256,2,4,128]{4,1,3,2,0:T(8,128)(2,1)}, u32[]{:S(2)}) copy-start(bf16[2,256,2,4,128]{4,1,3,2,0:T(8,128)(2,1)} %get-tuple-element.34) | copy-start | bytes 3145732 | tf_op jit(solution)/shard_map/cond
  513.0 0.7 copy-start.13
  513.7 45.6 %copy-start.1 = (bf16[4096,256]{1,0:T(8,128)(2,1)S(1)}, bf16[4096,256]{1,0:T(8,128)(2,1)}, u32[]{:S(2)}) copy-start(bf16[4096,256]{1,0:T(8,128)(2,1)} %param.21) | copy-start | bytes 6291460
Sparse Core Ops, SparseCore 0:
  9.7 40.3 all-gather.3
  60.7 144.8 all-gather.5
  207.8 166.0 all-gather.7
  513.2 40.6 reduce-scatter.1
where the time goes:
time: 567 us; the launch traced here: 566 us
  waiting for transfers between devices  364 us (64%)
  matrix products  126 us (22%)
  local copies, waits for them, and re-layouts  37.2 us (7%)
  other arithmetic  23.4 us (4%)
  between operations  14.7 us (3%)
    all_gather x1, waiting for transfers between devices, on_device(): lax.all_gather(clean_values, 'ctx', axis=0, tiled=True)  168 us
    all_gather x1, waiting for transfers between devices, on_device(): lax.all_gather(clean_keys, 'ctx', axis=0, tiled=True)  118 us
    dot_general x1, matrix products, compute(): jnp.einsum('srhgk,khd->srhgd', weights.astype(jnp.bfloat16), value_heads,...  56.5 us
    dot_general x1, matrix products, compute(): jnp.einsum('srhgd,khd->srhgk', queries, key_heads, preferred_element_type...  48.1 us
    reduce_scatter x1, waiting for transfers between devices, on_device(): lax.psum_scatter(jnp.dot(head_rows, w_out, preferred_element_type=jnp.flo...  40 us
    all_gather x1, waiting for transfers between devices, on_device(): features = lax.all_gather(clean_tokens, 'copy', axis=1, tiled=True)  36.6 us
    dot_general x1, local copies, waits for them, and re-layouts, on_device(): jnp.dot(all_rows, w_query, preferred_element_type=jnp.float32)  11.4 us
  transfers between devices with their start and end apart: 4, of which 4 were waited for; matrix products, arithmetic and copies ran while one was open for 6% of the time, Pallas kernels for 0%

commit v1 on v0

--- a/solution.py
+++ b/solution.py
@@ -8,6 +8,13 @@
 BLK = 64
 TSTEPS = 1000
 EPS = 1e-06
+
+
+def swapped_in(value, mesh_axis, d):
+    peers = lax.axis_size(mesh_axis)
+    blocks = jnp.stack([value for _ in range(peers)])
+    blocks = lax.all_to_all(blocks, mesh_axis, split_axis=0, concat_axis=0)
+    return jnp.concatenate(blocks, axis=d)
 
 
 def inverse_rms(values):
@@ -131,7 +138,7 @@
     )
     piece = (
         lax.all_gather(clean_keys, "ctx", axis=0, tiled=True),
-        lax.all_gather(clean_values, "ctx", axis=0, tiled=True),
+        swapped_in(clean_values, "ctx", 0),
     )
     key_start = jnp.int32(0)
     totals = tuple(

time: 567 us -> 427 us (0.75)
  waiting for transfers between devices: 364 us -> 215 us
  starting transfers between devices: 0.16 us -> 7.24 us
    all_gather x1 -> x0, waiting for transfers between devices: 168 us -> none  [on_device(): lax.all_gather(clean_values, 'ctx', axis=0, tiled=True)]
    all_to_all x0 -> x1, waiting for transfers between devices: none -> 83.8 us  [swapped_in(): blocks = lax.all_to_all(blocks, mesh_axis, split_axis=0, concat_axis=0)]
    all_gather x1, waiting for transfers between devices: 118 us -> 58.7 us  [on_device(): lax.all_gather(clean_keys, 'ctx', axis=0, tiled=True)]
    another operation x1 -> x3, local copies, waits for them, and re-layouts: 0.04 us -> 9.41 us  [the longest x1 6.94 us: key_terms(): value_heads = value_piece.reshape(piece_rows, kv_local, head_dim)]
    all_to_all x0 -> x1, starting transfers between devices: none -> 7.12 us  [swapped_in(): blocks = lax.all_to_all(blocks, mesh_axis, split_axis=0, concat_axis=0)]
    reshape x1 -> x0, local copies, waits for them, and re-layouts: 6.93 us -> none  [key_terms(): value_heads = value_piece.reshape(piece_rows, kv_local, head_dim)]
  transfers between devices with their start and end apart: 4 -> 4, of which waited for: 4 -> 4; matrix products, arithmetic and copies ran while one was open for 6% -> 8% of each run, Pallas kernels for 0% -> 0%
where the time goes in v1:
time: 427 us; the launch traced here: 426 us
  waiting for transfers between devices  215 us (50%)
  matrix products  126 us (30%)
  local copies, waits for them, and re-layouts  39.1 us (9%)
  other arithmetic  23.4 us (5%)
  between operations  14.7 us (3%)
  starting transfers between devices  7.24 us (2%)
    all_to_all x1, waiting for transfers between devices, swapped_in(): blocks = lax.all_to_all(blocks, mesh_axis, split_axis=0, concat_axis=0)  83.8 us
    all_gather x1, waiting for transfers between devices, on_device(): lax.all_gather(clean_keys, 'ctx', axis=0, tiled=True)  58.7 us
    dot_general x1, matrix products, compute(): jnp.einsum('srhgk,khd->srhgd', weights.astype(jnp.bfloat16), value_heads,...  56.5 us
    dot_general x1, matrix products, compute(): jnp.einsum('srhgd,khd->srhgk', queries, key_heads, preferred_element_type...  48.1 us
    all_gather x1, waiting for transfers between devices, on_device(): features = lax.all_gather(clean_tokens, 'copy', axis=1, tiled=True)  36.6 us
    reduce_scatter x1, waiting for transfers between devices, on_device(): lax.psum_scatter(jnp.dot(head_rows, w_out, preferred_element_type=jnp.flo...  35.1 us
    dot_general x1, local copies, waits for them, and re-layouts, on_device(): jnp.dot(all_rows, w_query, preferred_element_type=jnp.float32)  11.6 us
    dot_general x1, matrix products, on_device(): jnp.dot(head_rows, w_out, preferred_element_type=jnp.float32)  10.1 us
  transfers between devices with their start and end apart: 4, of which 4 were waited for; matrix products, arithmetic and copies ran while one was open for 8% of the time, Pallas kernels for 0%

profile of v1, /device:TPU:1, one launch (start us, length us, event | category | flops | bytes accessed | tf_op | source)
XLA Modules:
  0.0 425.8 jit_solution(3484438408404583273)
XLA Ops:
  9.3 4.1 copy.93
  13.5 36.6 %all-gather.3.cloned.1.call-done = bf16[256,4096]{1,0:T(8,128)(2,1)} async-done(((bf16[256,2048]{1,0:T(8,128)(2,1)}), bf16[256,4096]{1,0:T(8,128)(2,1)}) %all-gather.3.cloned.1.call-update) | async-done | bytes 2097168 | tf_op jit(solution)/shard_map/all_gather | solution.py:93
  50.1 3.4 fusion.19
  53.5 4.2 fusion.31
  57.7 1.3 multiply_reduce_fusion.1
  60.6 2.6 pad_maximum_fusion
  63.2 1.3 convolution_convert_fusion
  64.5 2.4 stack.3
  67.0 7.1 %all-to-all-start = ((bf16[32,256,256]{2,1,0:T(8,128)(2,1)}), bf16[32,256,256]{2,1,0:T(8,128)(2,1)}, u32[]{:S(2)}, u32[]{:S(2)}) async-start(bf16[32,256,256]{2,1,0:T(8,128)(2,1)} %stack.3), calls=%async_computation | async-start | bytes 8388608 | tf_op jit(solution)/shard_map/all_to_all | solution.py:16
  74.2 11.6 %copy.94 = bf16[1024,4096]{1,0:T(8,128)(2,1)} copy(bf16[1024,4096]{0,1:T(8,128)(2,1)} %bitcast.72) | data formatting | bytes 16777216 | tf_op jit(solution)/shard_map/dot_general | solution.py:115
  85.9 8.1 %multiply_reduce_fusion = (f32[2,256,2,4]{1,3,2,0:T(4,128)S(1)}, f32[2,256,2,4,128]{4,1,3,2,0:T(8,128)S(1)}) fusion(bf16[2,4,128,4096,1]{3,2,1,0,4:T(8,128)(2,1)} %bitcast.73, bf16[1,256,4096]{2,1,0:T(8,128)(2,1)} %copy-done.4, bf16[1,256,4096]{2,1,0:T(8,128)(2,1)S(1)} %copy-done.3), kind=kOutput, calls=%fused_computation.50 | convolution fusion | flops 4304400384 | bytes 14696448 | tf_op jit(solution)/shard_map/dot_general | solution.py:115
  96.2 83.8 %all-to-all-done = bf16[32,256,256]{2,1,0:T(8,128)(2,1)} async-done(((bf16[32,256,256]{2,1,0:T(8,128)(2,1)}), bf16[32,256,256]{2,1,0:T(8,128)(2,1)}, u32[]{:S(2)}, u32[]{:S(2)}) %all-to-all-start) | async-done | bytes 4194336 | tf_op jit(solution)/shard_map/all_to_all | solution.py:16
  180.0 58.7 %all-gather.5.cloned.1.call-done = bf16[8192,256]{1,0:T(8,128)(2,1)} async-done(((bf16[256,256]{1,0:T(8,128)(2,1)}), bf16[8192,256]{1,0:T(8,128)(2,1)}) %all-gather.5.cloned.1.call-update) | async-done | bytes 4194320 | tf_op jit(solution)/shard_map/all_gather | solution.py:140
  238.7 126.6 %conditional.1 = (f32[2,256,2,4,128]{4,1,3,0,2:T(8,128)S(1)}, f32[2,256,2,4]{1,3,0,2:T(4,128)S(1)}) conditional(s32[]{:T(128)} %convert_element_type.70, () %tuple.16, (s32[]{:T(128)}, bf16[8192,256]{1,0:T(8,128)(2,1)}, bf16[2,256,2,4,128]{4,1,3,2,0:T(8,128)(2,1)}, bf16[32,256,256]{2,1,0:T(8,128)(2,1)}) %tuple.43), branch_computations={%region_4.5_spmd, %region_5.7_spmd} | conditional | flops 17385472000 | bytes 313739328 | solution.py:52
  238.8 7.9 %broadcast_compare_fusion = pred[2,256,8192]{1,2,0:T(8,128)(4,1)} fusion(s32[256]{0:T(256)S(1)} %and_select_fusion, s32[2,8192]{1,0:T(2,128)S(1)} %broadcast_add_fusion), kind=kLoop, calls=%fused_computation.5 | loop fusion | flops 4194304 | bytes 4260864 | tf_op jit(solution)/shard_map/cond/branch_1_fun/le | solution.py:38
  246.7 7.0 %reshape.216 = bf16[8192,2,128]{2,1,0:T(2,128)(2,1)} reshape(bf16[8192,256]{1,0:T(8,128)(2,1)} %get-tuple-element.11) | data formatting | bytes 8388608 | tf_op jit(solution)/shard_map/reshape | solution.py:28
  253.7 48.1 %fusion = (f32[2,256,2,4]{1,3,0,2:T(4,128)S(1)}, f32[2,8192,2,256,4]{3,1,4,2,0:T(8,128)}) fusion(pred[2,256,8192]{1,2,0:T(8,128)(4,1)} %broadcast_compare_fusion, bf16[2,256,2,4,128]{4,1,3,2,0:T(8,128)(2,1)S(1)} %copy-done.6, bf16[8192,2,128,1,1]{2,1,0,4,3:T(2,128)(2,1)} %bitcast.74), kind=kOutput, calls=%fused_computation.1 | convolution fusion | flops 8690593792 | bytes 143671296 | tf_op jit(solution)/shard_map/cond/branch_1_fun/srhgd,khd->srhgk/dot_general | solution.py:32
  301.8 6.9 %reshape_reshape.3 = bf16[8192,2,128]{2,1,0:T(2,128)(2,1)} reshape(bf16[32,256,256]{2,1,0:T(8,128)(2,1)} %get-tuple-element.13) | data formatting | bytes 8388608 | tf_op jit(solution)/shard_map/reshape;reshape | solution.py:29
  308.7 56.5 %fusion.8 = f32[2,256,2,4,128]{4,1,3,0,2:T(8,128)S(1)} fusion(bf16[8192,2,128,1,1]{2,1,0,4,3:T(2,128)(2,1)} %bitcast.75, f32[2,8192,2,256,4]{3,1,4,2,0:T(8,128)} %get-tuple-element.39, pred[2,256,8192]{1,2,0:T(8,128)(4,1)} %broadcast_compare_fusion), kind=kOutput, calls=%fused_computation.9 | convolution fusion | flops 8690597888 | bytes 144703488 | tf_op jit(solution)/shard_map/cond/branch_1_fun/srhgk,khd->srhgd/dot_general | solution.py:40
  366.2 0.8 copy.80
  367.8 10.1 %fusion.47 = f32[512,4096]{1,0:T(8,128)} fusion(bf16[512,1024]{1,0:T(8,128)(2,1)S(1)} %convert_element_type.83, bf16[1024,4096]{1,0:T(8,128)(2,1)} %param.22), kind=kOutput, calls=%fused_computation.80 | convolution fusion | flops 4294967296 | bytes 17825792 | tf_op jit(solution)/shard_map/dot_general | solution.py:161
  378.7 35.1 %reduce-scatter.2.cloned.1.call-done = f32[512,2048]{1,0:T(8,128)} async-done(((f32[512,4096]{1,0:T(8,128)}), f32[512,2048]{1,0:T(8,128)}) %reduce-scatter.2.cloned.1.call-update) | async-done | bytes 4194320 | tf_op jit(solution)/shard_map/reduce_scatter | solution.py:160
  413.8 2.7 slice.66
  416.5 2.7 fusion.36
  (65 shorter events, 8.0 us)
Async XLA Ops:
  7.2 56.1 %copy-start = (bf16[4096,256]{1,0:T(8,128)(2,1)S(1)}, bf16[4096,256]{1,0:T(8,128)(2,1)}, u32[]{:S(2)}) copy-start(bf16[4096,256]{1,0:T(8,128)(2,1)} %param.21) | copy-start | bytes 6291460
  7.2 6.3 %copy-start.12 = (s32[1,256]{1,0:T(1,128)S(1)}, s32[1,256]{1,0:T(1,128)}, u32[]{:S(2)}) copy-start(s32[1,256]{1,0:T(1,128)} %param.25) | copy-start | bytes 3076
  7.2 6.3 %copy-start.9 = (f32[4096]{0:T(1024)S(1)}, f32[4096]{0:T(1024)}, u32[]{:S(2)}) copy-start(f32[4096]{0:T(1024)} %param.18) | copy-start | bytes 49156
  7.2 42.9 %copy-start.8 = (bf16[4096]{0:T(1024)(128)(2,1)S(1)}, bf16[4096]{0:T(1024)(128)(2,1)}, u32[]{:S(2)}) copy-start(bf16[4096]{0:T(1024)(128)(2,1)} %param.17) | copy-start | bytes 24580
  7.2 42.9 %all-gather.3.cloned.1.call-start = ((), (), s32[]{:S(2)}) async-start(), calls=%async_computation.2 | async-start | bytes 3145728 | tf_op jit(solution)/shard_map/all_gather | solution.py:93
  7.9 230.7 %all-gather.5.cloned.1.call-start = ((), (), s32[]{:S(2)}) async-start(), calls=%async_computation.3 | async-start | bytes 4325376 | tf_op jit(solution)/shard_map/all_gather | solution.py:140
  50.1 7.6 %copy-start.7 = (bf16[256,4096]{1,0:T(8,128)(2,1)S(1)}, bf16[256,4096]{1,0:T(8,128)(2,1)}, u32[]{:S(2)}) copy-start(bf16[256,4096]{1,0:T(8,128)(2,1)} %copy.93) | copy-start | bytes 6291460
  57.7 1.4 copy-start.2
  57.7 2.0 copy-start.4
  57.7 2.0 copy-start.10
  67.0 113.0 %all-to-all-start = ((bf16[32,256,256]{2,1,0:T(8,128)(2,1)}), bf16[32,256,256]{2,1,0:T(8,128)(2,1)}, u32[]{:S(2)}, u32[]{:S(2)}) async-start(bf16[32,256,256]{2,1,0:T(8,128)(2,1)} %stack.3), calls=%async_computation | async-start | bytes 8388608 | tf_op jit(solution)/shard_map/all_to_all | solution.py:16
  74.1 339.7 %reduce-scatter.2.cloned.1.call-start = ((), (), s32[]{:S(2)}) async-start(), calls=%async_computation.4 | async-start | bytes 12582912 | tf_op jit(solution)/shard_map/reduce_scatter | solution.py:160
  74.2 11.7 %copy-start.3 = (bf16[1,256,4096]{2,1,0:T(8,128)(2,1)S(1)}, bf16[1,256,4096]{2,1,0:T(8,128)(2,1)}, u32[]{:S(2)}) copy-start(bf16[1,256,4096]{2,1,0:T(8,128)(2,1)} %copy-done.2) | copy-start | bytes 6291460
  85.9 8.2 %copy-start.11 = (f32[128]{0:T(128)S(1)}, f32[128]{0:T(128)}, u32[]{:S(2)}) copy-start(f32[128]{0:T(128)} %param.23) | copy-start | bytes 1540
  94.8 1.0 copy-start.5
  246.7 7.0 %copy-start.6 = (bf16[2,256,2,4,128]{4,1,3,2,0:T(8,128)(2,1)S(1)}, bf16[2,256,2,4,128]{4,1,3,2,0:T(8,128)(2,1)}, u32[]{:S(2)}) copy-start(bf16[2,256,2,4,128]{4,1,3,2,0:T(8,128)(2,1)} %get-tuple-element.34) | copy-start | bytes 3145732 | tf_op jit(solution)/shard_map/cond
  377.8 0.7 copy-start.13
  378.5 40.7 %copy-start.1 = (bf16[4096,256]{1,0:T(8,128)(2,1)S(1)}, bf16[4096,256]{1,0:T(8,128)(2,1)}, u32[]{:S(2)}) copy-start(bf16[4096,256]{1,0:T(8,128)(2,1)} %param.21) | copy-start | bytes 6291460
Sparse Core Ops, SparseCore 0:
  9.7 40.3 all-gather.2
  60.7 177.8 all-gather.4
  378.0 35.7 reduce-scatter.1
